TPU v7x, 256 devices: a whole 4x4x8 slice. The times are simulated.
256 devices in a mesh: row: 8 (over y, core), col: 32 (over x, z).
Axes of the slice: x: 4, y: 4, z: 8, core: 2. Of those that a mesh axis runs over, the one named last changes fastest.
Arguments:
- sources: float32 [65536, 256], P(('row', 'col')), may hold values from -6 to 6
- targets: float32 [65536, 256], P(('col', 'row')), may hold values from -6 to 6
- g_pot: float32 [65536], P(('col', 'row')), may hold values from -1 to 12
- log_a: float32 [65536], P(('row', 'col')), may hold values from -14 to -8
- log_b: float32 [65536], P(('col', 'row')), may hold values from -14 to -8
- src_block: int32 [16384], P(('row', 'col')), may hold values from 0 to 31, as said below
- tgt_block: int32 [16384], P(('row', 'col')), may hold values from 0 to 7, as said below
- pair_count: int32 [256], P(('row', 'col')), may hold values from 16 to 64, as said below
Outputs:
- f_new: float32 [65536], P(('row', 'col'))
- g_new: float32 [65536], P(('col', 'row'))
Inputs may be any that keep to these rules, and one draw needn't show every extreme that they name: `src_block`: within each row index, slot 0 of the 32 devices names together every source block of that row index once; slot k and slot k + 32 of a device name the same source block. `tgt_block`: within each col index, slot 0 of the 8 devices names together every target block of that col index once. `pair_count`: some device has all 64 slots live.
All inputs are finite; a program needn't handle non-finite values.
Results may differ from a plain program's by a relative error of at most 0.0003.
Values sent between devices are 32-bit elements; how exact they have to be, the bound alone decides.
A program may use at most 128 MiB of HBM per device.

v0:
```python
import jax
import jax.numpy as jnp
from jax import lax
from jax.sharding import PartitionSpec as P

BLK = 256
entropy = 0.05
lowest = -1e30


def squares_of(rows):
    return jnp.sum(rows * rows, axis=-1)


def cost_blocks(src_rows, tgt_rows, src_sq, tgt_sq):
    inner = jnp.einsum("kid,kjd->kij", src_rows, tgt_rows, precision=lax.Precision.HIGHEST)
    return (src_sq[:, :, None] + tgt_sq[:, None, :] - 2.0 * inner) / src_rows.shape[2]


def fold_blocks(slot_top, slot_total, slot_ids, alive, count):
    onehot = (slot_ids[:, None] == jnp.arange(count, dtype=jnp.int32)[None, :]) & alive[:, None]
    masked = jnp.where(onehot.T[:, :, None], slot_top[None, :, :], lowest)
    top = jnp.max(masked, axis=1)
    back = jnp.take(top, slot_ids, axis=0)
    weighted = jnp.where(alive[:, None], slot_total * jnp.exp(slot_top - back), 0.0)
    total = jnp.dot(onehot.T.astype(jnp.float32), weighted, precision=lax.Precision.HIGHEST)
    return (top.reshape(-1), total.reshape(-1))


def local(sources, targets, g_pot, log_a, log_b, src_block, tgt_block, pair_count):
    used_pairs = pair_count[0]
    slots = src_block.shape[0]
    alive = jnp.arange(slots, dtype=jnp.int32) < used_pairs
    tgt_all, pot_all = (
        lax.all_gather(targets, "row", axis=0, tiled=True),
        lax.all_gather(g_pot, "row", axis=0, tiled=True),
    )
    src_all, weight_all = (
        lax.all_gather(sources, "col", axis=0, tiled=True),
        lax.all_gather(log_a, "col", axis=0, tiled=True),
    )
    width = sources.shape[1]
    src_count = src_all.shape[0] // BLK
    tgt_count = tgt_all.shape[0] // BLK
    src_blocks = src_all.reshape(src_count, BLK, width)
    tgt_blocks = tgt_all.reshape(tgt_count, BLK, width)
    src_sq_all = squares_of(src_blocks)
    tgt_sq_all = squares_of(tgt_blocks)
    src_rows = jnp.take(src_blocks, src_block, axis=0)
    tgt_rows = jnp.take(tgt_blocks, tgt_block, axis=0)
    src_sq = jnp.take(src_sq_all, src_block, axis=0)
    tgt_sq = jnp.take(tgt_sq_all, tgt_block, axis=0)
    pot_rows = jnp.take(pot_all.reshape(tgt_count, BLK), tgt_block, axis=0)
    costs = cost_blocks(src_rows, tgt_rows, src_sq, tgt_sq)
    scores = (pot_rows[:, None, :] - costs) / entropy
    slot_top = jnp.max(scores, axis=2)
    slot_total = jnp.sum(jnp.exp(scores - slot_top[:, :, None]), axis=2)
    src_top, src_total = fold_blocks(slot_top, slot_total, src_block, alive, src_count)
    whole_top = lax.pmax(src_top, "col")
    src_total = lax.psum(src_total * jnp.exp(src_top - whole_top), "col")
    src_top = whole_top
    f_all = entropy * weight_all - entropy * (src_top + jnp.log(src_total))
    second_costs = cost_blocks(src_rows, tgt_rows, src_sq, tgt_sq)
    f_rows = jnp.take(f_all.reshape(src_count, BLK), src_block, axis=0)
    back_scores = (f_rows[:, :, None] - second_costs) / entropy
    col_top = jnp.max(back_scores, axis=1)
    col_total = jnp.sum(jnp.exp(back_scores - col_top[:, None, :]), axis=1)
    tgt_top, tgt_total = fold_blocks(col_top, col_total, tgt_block, alive, tgt_count)
    whole_tgt = lax.pmax(tgt_top, "row")
    tgt_total = lax.psum(tgt_total * jnp.exp(tgt_top - whole_tgt), "row")
    tgt_top = whole_tgt
    own_src = sources.shape[0]
    own_tgt = targets.shape[0]
    f_own = lax.dynamic_slice_in_dim(f_all, lax.axis_index("col") * own_src, own_src, 0)
    tgt_offset = lax.axis_index("row") * own_tgt
    top_own = lax.dynamic_slice_in_dim(tgt_top, tgt_offset, own_tgt, 0)
    total_own = lax.dynamic_slice_in_dim(tgt_total, tgt_offset, own_tgt, 0)
    g_own = entropy * log_b - entropy * (top_own + jnp.log(total_own))
    return (f_own, g_own)


def solution(mesh):
    placed = (
        P(("row", "col"), None),
        P(("col", "row"), None),
        P(("col", "row")),
        P(("row", "col")),
        P(("col", "row")),
        P(("row", "col")),
        P(("row", "col")),
        P(("row", "col")),
    )
    return jax.shard_map(
        local,
        mesh=mesh,
        in_specs=placed,
        out_specs=(P(("row", "col")), P(("col", "row"))),
        check_vma=False,
    )
```

profile of v0, /device:TPU:1, one launch (start us, length us, event | category | flops | bytes accessed | tf_op | source)
XLA Modules:
  0.0 527.1 jit_solution(1191801241612126786)
XLA Ops:
  7.2 0.7 all-gather.7.cloned.1.call-update
  7.9 0.7 all-gather.5.cloned.1.call-update
  8.7 12.4 %all-gather.1 = f32[8,1,256]{2,1,0:T(1,128)S(1)} all-gather(f32[1,1,256]{2,1,0:T(1,128)} %bitcast.32), channel_id=1, replica_groups=mesh['row'=8,'col'=32] {'row'}, dimensions={0}, use_global_device_ids=true | all-gather | bytes 9216 | tf_op jit(solution)/shard_map/all_gather | solution.py:36
  21.7 0.7 compare_select_fusion.1
  23.0 37.7 %all-gather = f32[32,1,256]{2,1,0:T(1,128)S(1)} all-gather(f32[1,1,256]{2,1,0:T(1,128)} %bitcast.33), channel_id=1, replica_groups=mesh['row'=8,'col'=32] {'col'}, dimensions={0}, use_global_device_ids=true | all-gather | bytes 33792 | tf_op jit(solution)/shard_map/all_gather | solution.py:40
  60.8 0.7 compare_select_fusion
  61.4 0.7 compare_and_fusion.1
  62.1 0.7 compare_and_fusion
  62.8 0.7 fusion.37
  63.4 0.7 fusion.36
  64.2 1.9 multiply_reduce_fusion.1
  66.1 0.7 gather_fusion.4
  66.8 10.5 %gather_fusion.1 = f32[64,256,256]{2,1,0:T(8,128)} fusion(f32[8,256,256]{2,1,0:T(8,128)} %bitcast.20, s32[1024]{0:T(1024)S(1)} %pad_clamp_fusion.1), kind=kCustom, calls=%fused_computation.7 | custom fusion | bytes 33554688 | tf_op jit(solution)/shard_map/jit(_take)/gather | solution.py:50
  77.3 64.3 %all-gather.5.cloned.1.call-done = f32[8192,256]{1,0:T(8,128)} async-done(((f32[256,256]{1,0:T(8,128)}), f32[8192,256]{1,0:T(8,128)}) %all-gather.5.cloned.1.call-update) | async-done | bytes 8388624 | tf_op jit(solution)/shard_map/all_gather | solution.py:39
  141.6 4.5 multiply_reduce_fusion
  146.8 11.6 %gather_fusion = f32[64,256,256]{2,1,0:T(8,128)} fusion(f32[32,256,256]{2,1,0:T(8,128)} %bitcast.21, s32[1024]{0:T(1024)S(1)} %pad_clamp_fusion), kind=kCustom, calls=%fused_computation.6 | custom fusion | bytes 33554688 | tf_op jit(solution)/shard_map/jit(_take)/gather | solution.py:49
  158.5 29.9 %fusion.3 = (f32[64,256]{1,0:T(8,128)S(1)}, f32[64,256,256]{2,1,0:T(8,128)}) fusion(f32[64,256]{1,0:T(8,128)S(1)} %get-tuple-element.4, f32[64,256,256]{2,1,0:T(8,128)} %gather_fusion.1, pred[64]{0:T(512)(128)(4,1)S(1)} %compare_and_fusion.1, f32[64,256,256]{2,1,0:T(8,128)} %gather_fusion, pred[64]{0:T(512)(128)(4,1)S(1)} %compare_and_fusion, ...), kind=kOutput, calls=%fused_computation.16 | convolution fusion | flops 12922634240 | bytes 50593920 | tf_op jit(solution)/shard_map/kid,kjd->kij/dot_general | solution.py:16
  188.4 8.5 %exponential_reduce_fusion.1 = f32[64,256]{1,0:T(8,128)S(1)} fusion(f32[64,256,256]{2,1,0:T(8,128)} %get-tuple-element.7, f32[64,256]{1,0:T(8,128)S(1)} %get-tuple-element.6, f32[64,256]{1,0:T(8,128)S(1)} %get-tuple-element.4), kind=kLoop, calls=%fused_computation.10 | loop fusion | flops 16760832 | bytes 16973824 | tf_op jit(solution)/shard_map/reduce_sum | solution.py:57
  198.5 111.5 %pmax.14 = f32[8192]{0:T(1024)S(1)} all-reduce(f32[8192]{0:T(1024)S(1)} %bitcast.25), channel_id=1, replica_groups=mesh['row'=8,'col'=32] {'col'}, use_global_device_ids=true, to_apply=%region_4.7 | all-reduce | flops 8192 | bytes 65536 | tf_op jit(solution)/shard_map/pmax | solution.py:59
  310.0 110.7 %psum.14 = f32[8192]{0:T(1024)S(1)} all-reduce(f32[8192]{0:T(1024)S(1)} %exponential_multiply_fusion), channel_id=1, replica_groups=mesh['row'=8,'col'=32] {'col'}, use_global_device_ids=true, to_apply=%region_6.9 | all-reduce | flops 8192 | bytes 65536 | tf_op jit(solution)/shard_map/psum | solution.py:60
  421.5 7.2 %fusion.4 = f32[64,256]{1,0:T(8,128)S(1)} fusion(f32[64,256,256]{2,1,0:T(8,128)} %get-tuple-element.7, f32[64,256]{1,0:T(8,128)S(1)} %broadcast_select_fusion), kind=kLoop, calls=%fused_computation.17 | loop fusion | flops 12566528 | bytes 16908288 | tf_op jit(solution)/shard_map/reduce_max | solution.py:66
  428.8 8.0 %exponential_reduce_fusion = f32[64,256]{1,0:T(8,128)S(1)} fusion(f32[64,256,256]{2,1,0:T(8,128)} %get-tuple-element.7, f32[64,256]{1,0:T(8,128)S(1)} %fusion.4, f32[64,256]{1,0:T(8,128)S(1)} %broadcast_select_fusion), kind=kLoop, calls=%fused_computation.8 | loop fusion | flops 16760832 | bytes 16973824 | tf_op jit(solution)/shard_map/reduce_sum | solution.py:67
  437.9 68.4 %pmax.15 = f32[2048]{0:T(1024)S(1)} all-reduce(f32[2048]{0:T(1024)S(1)} %bitcast.29), channel_id=1, replica_groups=mesh['row'=8,'col'=32] {'row'}, use_global_device_ids=true, to_apply=%region_9.12 | all-reduce | flops 2048 | bytes 16384 | tf_op jit(solution)/shard_map/pmax | solution.py:69
  506.3 12.7 %psum.15 = f32[2048]{0:T(1024)S(1)} all-reduce(f32[2048]{0:T(1024)S(1)} %exponential_multiply_fusion.1), channel_id=1, replica_groups=mesh['row'=8,'col'=32] {'row'}, use_global_device_ids=true, to_apply=%region_11.14 | all-reduce | flops 2048 | bytes 16384 | tf_op jit(solution)/shard_map/psum | solution.py:70
  (38 shorter events, 6.3 us)
Async XLA Ops:
  7.2 57.0 %all-gather.7.cloned.1.call-start = ((), (), s32[]{:S(2)}) async-start(), calls=%async_computation.1 | async-start | bytes 2359296 | tf_op jit(solution)/shard_map/all_gather | solution.py:35
  7.9 133.7 %all-gather.5.cloned.1.call-start = ((), (), s32[]{:S(2)}) async-start(), calls=%async_computation | async-start | bytes 8650752 | tf_op jit(solution)/shard_map/all_gather | solution.py:39
  188.4 9.7 %copy-start.1 = (s32[64]{0:T(128)S(1)}, s32[64]{0:T(128)}, u32[]{:S(2)}) copy-start(s32[64]{0:T(128)} %param.17) | copy-start | bytes 772
  421.5 16.1 %copy-start.2 = (s32[64]{0:T(128)S(1)}, s32[64]{0:T(128)}, u32[]{:S(2)}) copy-start(s32[64]{0:T(128)} %param.18) | copy-start | bytes 772
  421.5 98.1 %copy-start = (f32[256]{0:T(256)S(1)}, f32[256]{0:T(256)}, u32[]{:S(2)}) copy-start(f32[256]{0:T(256)} %param.16) | copy-start | bytes 3076
Sparse Core Ops, SparseCore 0:
  9.8 32.0 all-gather.6
  44.5 97.0 all-gather.4
where the time goes:
time: 528 us; the launch traced here: 527 us
  blocking collectives  353 us (67%)
  waiting for transfers between devices  65.7 us (12%)
  other arithmetic  35.9 us (7%)
  matrix products  30.4 us (6%)
  local copies, waits for them, and re-layouts  26.8 us (5%)
  between operations  14.9 us (3%)
    pmax x1, blocking collectives, local(): whole_top = lax.pmax(src_top, 'col')  112 us
    psum x1, blocking collectives, local(): src_total = lax.psum(src_total * jnp.exp(src_top - whole_top), 'col')  111 us
    pmax x1, blocking collectives, local(): whole_tgt = lax.pmax(tgt_top, 'row')  68.4 us
    all_gather x1, waiting for transfers between devices, local(): lax.all_gather(sources, 'col', axis=0, tiled=True)  64.3 us
    all_gather x1, blocking collectives, local(): lax.all_gather(log_a, 'col', axis=0, tiled=True)  37.7 us
    dot_general x1, matrix products, cost_blocks(): jnp.einsum('kid,kjd->kij', src_rows, tgt_rows, precision=lax.Precision.HI...  29.9 us
    psum x1, blocking collectives, local(): tgt_total = lax.psum(tgt_total * jnp.exp(tgt_top - whole_tgt), 'row')  12.7 us
    all_gather x1, blocking collectives, local(): lax.all_gather(g_pot, 'row', axis=0, tiled=True)  12.4 us
  transfers between devices with their start and end apart: 2, of which 1 were waited for; matrix products, arithmetic and copies ran while one was open for 3% of the time, Pallas kernels for 0%

commit v1 on v0

--- a/solution.py
+++ b/solution.py
@@ -36,7 +36,9 @@
         lax.all_gather(g_pot, "row", axis=0, tiled=True),
     )
     src_all, weight_all = (
-        lax.all_gather(sources, "col", axis=0, tiled=True),
+        jnp.concatenate(
+            lax.all_to_all(jnp.stack([sources] * lax.axis_size("col")), "col", 0, 0), axis=0
+        ),
         lax.all_gather(log_a, "col", axis=0, tiled=True),
     )
     width = sources.shape[1]

time: 528 us -> 647 us (1.23)
  blocking collectives: 353 us -> 525 us
  waiting for transfers between devices: 65.7 us -> 0.7 us
  starting transfers between devices: 0.08 us -> 12 us
    all_gather x1, blocking collectives: 37.7 us -> 201 us  [local(): lax.all_gather(log_a, 'col', axis=0, tiled=True)]
    all_gather x1 -> x0, waiting for transfers between devices: 64.3 us -> none  [local(): lax.all_gather(sources, 'col', axis=0, tiled=True)]
    all_to_all x0 -> x1, starting transfers between devices: none -> 12 us  [local(): lax.all_to_all(jnp.stack([sources] * lax.axis_size('col')), 'col', 0, 0)]
    pmax x1, blocking collectives: 68.4 us -> 76.2 us  [local(): whole_tgt = lax.pmax(tgt_top, 'row')]
  transfers between devices with their start and end apart: 2 -> 2, of which waited for: 1 -> 0; matrix products, arithmetic and copies ran while one was open for 3% -> 2% of each run, Pallas kernels for 0% -> 0%
where the time goes in v1:
time: 647 us
  blocking collectives  525 us (81%)
  other arithmetic  31.9 us (5%)
  local copies, waits for them, and re-layouts  31.8 us (5%)
  matrix products  30.4 us (5%)
  between operations  15 us (2%)
  starting transfers between devices  12 us (2%)
    all_gather x1, blocking collectives, local(): lax.all_gather(log_a, 'col', axis=0, tiled=True)  201 us
    pmax x1, blocking collectives, local(): whole_top = lax.pmax(src_top, 'col')  113 us
    psum x1, blocking collectives, local(): src_total = lax.psum(src_total * jnp.exp(src_top - whole_top), 'col')  111 us
    pmax x1, blocking collectives, local(): whole_tgt = lax.pmax(tgt_top, 'row')  76.2 us
    dot_general x1, matrix products, cost_blocks(): jnp.einsum('kid,kjd->kij', src_rows, tgt_rows, precision=lax.Precision.HI...  29.9 us
  transfers between devices with their start and end apart: 2, of which 0 were waited for; matrix products, arithmetic and copies ran while one was open for 2% of the time, Pallas kernels for 0%

profile of v1, /device:TPU:1, one launch (start us, length us, event | category | flops | bytes accessed | tf_op | source)
XLA Modules:
  0.0 646.6 jit_solution(660882143342436884)
XLA Ops:
  7.2 5.1 stack.2
  12.3 12.0 %all-to-all-start = ((f32[32,256,256]{2,1,0:T(8,128)}), f32[32,256,256]{2,1,0:T(8,128)}, u32[]{:S(2)}, u32[]{:S(2)}) async-start(f32[32,256,256]{2,1,0:T(8,128)} %stack.2), calls=%async_computation | async-start | bytes 16777216 | tf_op jit(solution)/shard_map/all_to_all | solution.py:40
  24.4 0.7 all-gather.4.cloned.1.call-update
  25.1 11.6 %all-gather.1 = f32[8,1,256]{2,1,0:T(1,128)S(1)} all-gather(f32[1,1,256]{2,1,0:T(1,128)S(1)} %bitcast.30), channel_id=1, replica_groups=mesh['row'=8,'col'=32] {'row'}, dimensions={0}, use_global_device_ids=true | all-gather | bytes 9216 | tf_op jit(solution)/shard_map/all_gather | solution.py:36
  37.4 0.7 gather_fusion.2
  38.1 200.9 %all-gather = f32[32,1,256]{2,1,0:T(1,128)S(1)} all-gather(f32[1,1,256]{2,1,0:T(1,128)S(1)} %bitcast.31), channel_id=1, replica_groups=mesh['row'=8,'col'=32] {'col'}, dimensions={0}, use_global_device_ids=true | all-gather | bytes 33792 | tf_op jit(solution)/shard_map/all_gather | solution.py:42
  239.2 1.9 multiply_reduce_fusion.1
  241.1 0.7 gather_fusion.4
  241.8 10.4 %gather_fusion.1 = f32[64,256,256]{2,1,0:T(8,128)} fusion(f32[8,256,256]{2,1,0:T(8,128)} %bitcast.19, s32[1024]{0:T(1024)S(1)} %pad_clamp_fusion.1), kind=kCustom, calls=%fused_computation.7 | custom fusion | bytes 33554688 | tf_op jit(solution)/shard_map/jit(_take)/gather | solution.py:52
  252.3 4.5 multiply_reduce_fusion
  256.8 0.7 gather_fusion.3
  257.5 11.6 %gather_fusion = f32[64,256,256]{2,1,0:T(8,128)} fusion(f32[32,256,256]{2,1,0:T(8,128)} %all-to-all-done, s32[1024]{0:T(1024)S(1)} %pad_clamp_fusion), kind=kCustom, calls=%fused_computation.6 | custom fusion | bytes 33554688 | tf_op jit(solution)/shard_map/jit(_take)/gather | solution.py:51
  269.2 29.9 %fusion.3 = (f32[64,256]{1,0:T(8,128)S(1)}, f32[64,256,256]{2,1,0:T(8,128)}) fusion(f32[64,256]{1,0:T(8,128)S(1)} %get-tuple-element.4, f32[64,256,256]{2,1,0:T(8,128)} %gather_fusion.1, pred[64]{0:T(512)(128)(4,1)S(1)} %compare_and_fusion.1, f32[64,256,256]{2,1,0:T(8,128)} %gather_fusion, pred[64]{0:T(512)(128)(4,1)S(1)} %compare_and_fusion, ...), kind=kOutput, calls=%fused_computation.16 | convolution fusion | flops 12922634240 | bytes 50593920 | tf_op jit(solution)/shard_map/kid,kjd->kij/dot_general | solution.py:16
  299.1 8.5 %exponential_reduce_fusion.1 = f32[64,256]{1,0:T(8,128)S(1)} fusion(f32[64,256,256]{2,1,0:T(8,128)} %get-tuple-element.7, f32[64,256]{1,0:T(8,128)S(1)} %get-tuple-element.6, f32[64,256]{1,0:T(8,128)S(1)} %get-tuple-element.4), kind=kLoop, calls=%fused_computation.10 | loop fusion | flops 16760832 | bytes 16973824 | tf_op jit(solution)/shard_map/reduce_sum | solution.py:59
  308.1 0.7 gather_fusion.5
  309.1 112.5 %pmax.14 = f32[8192]{0:T(1024)S(1)} all-reduce(f32[8192]{0:T(1024)S(1)} %bitcast.23), channel_id=1, replica_groups=mesh['row'=8,'col'=32] {'col'}, use_global_device_ids=true, to_apply=%region_4.7 | all-reduce | flops 8192 | bytes 65536 | tf_op jit(solution)/shard_map/pmax | solution.py:61
  421.6 110.7 %psum.14 = f32[8192]{0:T(1024)S(1)} all-reduce(f32[8192]{0:T(1024)S(1)} %exponential_multiply_fusion), channel_id=1, replica_groups=mesh['row'=8,'col'=32] {'col'}, use_global_device_ids=true, to_apply=%region_6.9 | all-reduce | flops 8192 | bytes 65536 | tf_op jit(solution)/shard_map/psum | solution.py:62
  532.4 0.7 gather_fusion.6
  533.2 7.2 %fusion.4 = f32[64,256]{1,0:T(8,128)S(1)} fusion(f32[64,256,256]{2,1,0:T(8,128)} %get-tuple-element.7, f32[64,256]{1,0:T(8,128)S(1)} %broadcast_select_fusion), kind=kLoop, calls=%fused_computation.17 | loop fusion | flops 12566528 | bytes 16908288 | tf_op jit(solution)/shard_map/reduce_max | solution.py:68
  540.4 8.0 %exponential_reduce_fusion = f32[64,256]{1,0:T(8,128)S(1)} fusion(f32[64,256,256]{2,1,0:T(8,128)} %get-tuple-element.7, f32[64,256]{1,0:T(8,128)S(1)} %fusion.4, f32[64,256]{1,0:T(8,128)S(1)} %broadcast_select_fusion), kind=kLoop, calls=%fused_computation.8 | loop fusion | flops 16760832 | bytes 16973824 | tf_op jit(solution)/shard_map/reduce_sum | solution.py:69
  548.6 0.7 gather_fusion.7
  549.5 76.2 %pmax.15 = f32[2048]{0:T(1024)S(1)} all-reduce(f32[2048]{0:T(1024)S(1)} %bitcast.27), channel_id=1, replica_groups=mesh['row'=8,'col'=32] {'row'}, use_global_device_ids=true, to_apply=%region_9.12 | all-reduce | flops 2048 | bytes 16384 | tf_op jit(solution)/shard_map/pmax | solution.py:71
  625.8 12.7 %psum.15 = f32[2048]{0:T(1024)S(1)} all-reduce(f32[2048]{0:T(1024)S(1)} %exponential_multiply_fusion.1), channel_id=1, replica_groups=mesh['row'=8,'col'=32] {'row'}, use_global_device_ids=true, to_apply=%region_11.14 | all-reduce | flops 2048 | bytes 16384 | tf_op jit(solution)/shard_map/psum | solution.py:72
  639.1 0.6 multiply_subtract_fusion.1
  (41 shorter events, 2.4 us)
Async XLA Ops:
  7.2 17.9 %copy-start = (f32[256]{0:T(256)S(1)}, f32[256]{0:T(256)}, u32[]{:S(2)}) copy-start(f32[256]{0:T(256)} %param.14) | copy-start | bytes 3076
  7.2 30.2 %copy-start.4 = (s32[64]{0:T(128)S(1)}, s32[64]{0:T(128)}, u32[]{:S(2)}) copy-start(s32[64]{0:T(128)} %param.18) | copy-start | bytes 772
  7.2 30.9 %copy-start.1 = (f32[256]{0:T(256)S(1)}, f32[256]{0:T(256)}, u32[]{:S(2)}) copy-start(f32[256]{0:T(256)} %param.15) | copy-start | bytes 3076
  7.2 231.8 %copy-start.3 = (s32[64]{0:T(128)S(1)}, s32[64]{0:T(128)}, u32[]{:S(2)}) copy-start(s32[64]{0:T(128)} %param.17) | copy-start | bytes 772
  12.3 239.9 %all-to-all-start = ((f32[32,256,256]{2,1,0:T(8,128)}), f32[32,256,256]{2,1,0:T(8,128)}, u32[]{:S(2)}, u32[]{:S(2)}) async-start(f32[32,256,256]{2,1,0:T(8,128)} %stack.2), calls=%async_computation | async-start | bytes 16777216 | tf_op jit(solution)/shard_map/all_to_all | solution.py:40
  24.3 214.8 %all-gather.4.cloned.1.call-start = ((), (), s32[]{:S(2)}) async-start(), calls=%async_computation.1 | async-start | bytes 2359296 | tf_op jit(solution)/shard_map/all_gather | solution.py:35
  533.1 105.9 %copy-start.2 = (f32[256]{0:T(256)S(1)}, f32[256]{0:T(256)}, u32[]{:S(2)}) copy-start(f32[256]{0:T(256)} %param.16) | copy-start | bytes 3076
Sparse Core Ops, SparseCore 0:
  27.0 29.9 all-gather.3
